TPU v7x, 32 devices: a whole 2x2x4 slice. The times are simulated.
32 devices in a mesh: atoms: 8 (over z, y), sig: 4 (over x, core).
Axes of the slice: x: 2, y: 2, z: 4, core: 2. Of those that a mesh axis runs over, the one named last changes fastest.
Arguments:
- signals: bfloat16 [1024, 512], P(None, 'sig'), may hold values from -6 to 6
- dictionary: bfloat16 [1024, 4096], P(None, ('atoms', 'sig')), may hold values from -0.1875 to 0.1875
- selected: int32 [2, 4], P(None, 'sig'), may hold values from 0 to 63
- inverses: bfloat16 [2, 4, 64, 64], P(None, 'sig'), may hold values from -0.14 to 1.14
Outputs:
- correlations: bfloat16 [4096, 512], P('atoms', 'sig')
- coefficients: bfloat16 [2, 64, 512], P(None, None, 'sig')
- peak: float32 [512], P('sig')
All inputs are finite; a program needn't handle non-finite values.
Results may differ from a plain program's by a relative error of at most 0.006.
Values may be sent and summed in bfloat16 or wider, within the bound.
No kernel may reach another device: no remote copies, remote signals or barrier semaphores. Data moves between devices by JAX's collectives and lax.ppermute only.
A program may use at most 128 MiB of HBM per device.

v0:
```python
import jax
import jax.numpy as jnp
from jax import lax
from jax.sharding import PartitionSpec as P

BLK = 64
SB = 128
STEPS = 2


def spread(block, axis, holder):
    block = jnp.where(lax.axis_index(axis) == holder, block, jnp.zeros_like(block))
    return lax.psum(block, axis)


def shards(signals, dictionary, selected, inverses):
    gathered = lax.all_gather(dictionary, "sig", axis=1, tiled=True)
    width = gathered.shape[1]
    blocks_here = width // BLK
    block_total = signals.shape[1] // SB
    correlation = lax.dot_general(
        gathered, signals, (((0,), (0,)), ((), ())), preferred_element_type=jnp.float32
    )
    coefficients = jnp.zeros((STEPS, BLK, signals.shape[1]), jnp.bfloat16)

    def locate(step, slot):
        block_id = selected[step, slot]
        owner_index = block_id // blocks_here
        offset = block_id % blocks_here * BLK
        return (owner_index, offset)

    def panel_of(atom_block):
        return lax.dot_general(
            gathered, atom_block, (((0,), (0,)), ((), ())), preferred_element_type=jnp.float32
        ).astype(jnp.bfloat16)

    def refit(step, slot, rows_block):
        return jnp.dot(
            inverses[step, slot].astype(jnp.float32),
            rows_block,
            precision=lax.Precision.HIGHEST,
            preferred_element_type=jnp.float32,
        ).astype(jnp.bfloat16)

    def solve_block(correlation, step, slot, offset):
        rows_block = lax.dynamic_slice(correlation, (offset, slot * SB), (BLK, SB))
        return refit(step, slot, rows_block)

    def apply_block(correlation, coefficients, gram_panel, weights_block, step, slot):
        column_start = slot * SB
        columns = correlation
        columns = columns - jnp.dot(gram_panel, weights_block, preferred_element_type=jnp.float32)
        correlation = columns
        coefficients = lax.dynamic_update_slice(
            coefficients, weights_block[None], (step, 0, column_start)
        )
        return (correlation, coefficients)

    for step in range(STEPS):

        def advance(slot, carried):
            correlation, coefficients = carried
            owner_index, offset = locate(step, slot)
            atom_block = lax.dynamic_slice_in_dim(gathered, offset, BLK, 1)
            weights_block = solve_block(correlation, step, slot, offset)
            atom_block, weights_block = (
                spread(atom_block, "atoms", owner_index),
                spread(weights_block, "atoms", owner_index),
            )
            gram_panel = panel_of(atom_block)
            return apply_block(correlation, coefficients, gram_panel, weights_block, step, slot)

        correlation, coefficients = lax.fori_loop(
            0, block_total, advance, (correlation, coefficients)
        )
    largest = lax.pmax(jnp.max(jnp.abs(correlation), axis=0), "atoms")
    return (correlation.astype(jnp.bfloat16), coefficients, largest)


def solution(mesh):
    placed = (P(None, "sig"), P(None, ("atoms", "sig")), P(None, "sig"), P(None, "sig", None, None))
    return jax.shard_map(
        shards,
        mesh=mesh,
        in_specs=placed,
        out_specs=(P("atoms", "sig"), P(None, None, "sig"), P("sig")),
        check_vma=False,
    )
```

profile of v0, /device:TPU:0, one launch (start us, length us, event | category | flops | bytes accessed | tf_op | source)
XLA Modules:
  0.0 168.5 jit_solution(2854032412302445752)
XLA Ops:
  7.2 0.0 copy-start
  7.2 0.0 copy-start.4
  7.2 0.0 all-gather.2.cloned.1.call-start
  7.2 0.7 all-gather.2.cloned.1.call-update
  7.9 0.0 all-reduce.3.cloned.1.call-start
  8.0 0.0 copy-done.4
  8.0 0.6 fusion.12
  13.8 15.3 %all-gather.2.cloned.1.call-done = bf16[1024,512]{1,0:T(8,128)(2,1)} async-done(((bf16[1024,128]{1,0:T(8,128)(2,1)}), bf16[1024,512]{1,0:T(8,128)(2,1)}) %all-gather.2.cloned.1.call-update) | async-done | bytes 1048592 | tf_op jit(solution)/shard_map/all_gather | solution.py:17
  29.1 0.0 copy-start.1
  29.2 2.2 %dynamic-slice_select_fusion = (bf16[1024,64]{1,0:T(8,128)(2,1)}, bf16[1024,64]{1,0:T(8,128)(2,1)}) fusion(bf16[1024,512]{1,0:T(8,128)(2,1)} %all-gather.2.cloned.1.call-done, s32[]{:T(128)S(6)} %select_n.99, pred[]{:T(512)S(6)} %eq.16, s32[]{:T(128)S(6)} %select_n.91, pred[]{:T(512)S(6)} %eq.15), kind=kLoop, calls=%fused_computation.11 | loop fusion | flops 131072 | bytes 524298 | tf_op jit(solution)/shard_map/while/body/eval_jaxpr/jit(_where)/select_n | solution.py:12
  31.3 0.0 all-reduce.3.cloned.1.call-update
  31.3 0.0 copy-done
  31.3 0.0 copy-done.1
  31.4 0.0 copy-start.3
  31.4 0.5 fusion.13
  31.8 0.3 copy-done.3
  32.1 0.2 fusion.1
  32.3 37.3 %psum.33 = bf16[64,128]{1,0:T(8,128)(2,1)S(1)} all-reduce(bf16[64,128]{1,0:T(8,128)(2,1)S(1)} %fusion.1), channel_id=1, replica_groups=mesh['atoms'=8,'sig'=4] {'atoms'}, use_global_device_ids=true, to_apply=%region_1.2 | all-reduce | flops 8192 | bytes 32768 | tf_op jit(solution)/shard_map/while/body/eval_jaxpr/psum | solution.py:13
  69.5 35.7 %all-reduce.3.cloned.1.call-done = (bf16[1024,64]{1,0:T(8,128)(2,1)}, bf16[1024,64]{1,0:T(8,128)(2,1)}) async-done(((bf16[1024,64]{1,0:T(8,128)(2,1)}, bf16[1024,64]{1,0:T(8,128)(2,1)}), (bf16[1024,64]{1,0:T(8,128)(2,1)}, bf16[1024,64]{1,0:T(8,128)(2,1)})) %all-reduce.3.cloned.1.call-update) | async-done | bytes 262160 | tf_op jit(solution)/shard_map/while/body/eval_jaxpr/psum | solution.py:13
  105.2 0.0 copy-start.2
  105.2 1.5 convolution_subtract_fusion.1
  106.7 0.2 fusion.3
  106.9 35.4 %psum.35 = bf16[64,128]{1,0:T(8,128)(2,1)S(1)} all-reduce(bf16[64,128]{1,0:T(8,128)(2,1)S(1)} %fusion.3), channel_id=1, replica_groups=mesh['atoms'=8,'sig'=4] {'atoms'}, use_global_device_ids=true, to_apply=%region_3.4 | all-reduce | flops 8192 | bytes 32768 | tf_op jit(solution)/shard_map/while/body/eval_jaxpr/psum | solution.py:13
  142.3 0.0 copy-done.2
  142.3 1.2 abs_reduce_fusion
  143.4 17.6 %pmax.7 = f32[128]{0:T(128)} all-reduce(f32[128]{0:T(128)S(1)} %get-tuple-element.42), channel_id=1, replica_groups=mesh['atoms'=8,'sig'=4] {'atoms'}, use_global_device_ids=true, to_apply=%region_5.6 | all-reduce | flops 128 | bytes 1024 | tf_op jit(solution)/shard_map/pmax | solution.py:76
  161.1 0.6 pad_maximum_fusion
Async XLA Ops:
  7.2 24.2 %copy-start = (bf16[1024,128]{1,0:T(8,128)(2,1)S(1)}, bf16[1024,128]{1,0:T(8,128)(2,1)}, u32[]{:S(2)}) copy-start(bf16[1024,128]{1,0:T(8,128)(2,1)} %param.4) | copy-start | bytes 786436
  7.2 0.8 copy-start.4
  7.2 22.0 %all-gather.2.cloned.1.call-start = ((), (), s32[]{:S(2)}) async-start(), calls=%async_computation | async-start | bytes 1310720 | tf_op jit(solution)/shard_map/all_gather | solution.py:17
  7.9 97.3 %all-reduce.3.cloned.1.call-start = ((), (), s32[]{:S(2)}) async-start(), calls=%async_computation.1 | async-start | bytes 1048576 | tf_op jit(solution)/shard_map/while/body/eval_jaxpr/psum | solution.py:13
  29.1 2.2 %copy-start.1 = (bf16[1024,512]{1,0:T(8,128)(2,1)S(1)}, bf16[1024,512]{1,0:T(8,128)(2,1)}, u32[]{:S(2)}) copy-start(bf16[1024,512]{1,0:T(8,128)(2,1)} %all-gather.2.cloned.1.call-done) | copy-start | bytes 3145732
  31.4 0.8 copy-start.3
  105.2 37.0 %copy-start.2 = (bf16[1024,64]{1,0:T(8,128)(2,1)S(1)}, bf16[1024,64]{1,0:T(8,128)(2,1)}, u32[]{:S(2)}) copy-start(bf16[1024,64]{1,0:T(8,128)(2,1)} %get-tuple-element.32) | copy-start | bytes 393220
Sparse Core Ops, SparseCore 0:
  9.6 19.5 all-gather.1
  32.6 72.5 all-reduce.2
where the time goes:
time: 169 us
  blocking collectives  90.2 us (53%)
  waiting for transfers between devices  51.7 us (31%)
  between operations  19.3 us (11%)
  matrix products  3.47 us (2%)
  other arithmetic  2.78 us (2%)
    psum x2, blocking collectives, spread(): return lax.psum(block, axis)  72.6 us
    psum x1, waiting for transfers between devices, spread(): return lax.psum(block, axis)  35.7 us
    pmax x1, blocking collectives, shards(): largest = lax.pmax(jnp.max(jnp.abs(correlation), axis=0), 'atoms')  17.6 us
    all_gather x1, waiting for transfers between devices, shards(): gathered = lax.all_gather(dictionary, 'sig', axis=1, tiled=True)  15.3 us
  transfers between devices with their start and end apart: 2, of which 2 were waited for; matrix products, arithmetic and copies ran while one was open for 1% of the time, Pallas kernels for 0%

commit v1 on v0

--- a/solution.py
+++ b/solution.py
@@ -10,7 +10,11 @@
 
 def spread(block, axis, holder):
     block = jnp.where(lax.axis_index(axis) == holder, block, jnp.zeros_like(block))
-    return lax.psum(block, axis)
+
+    def _start_paths(local_block):
+        return jax.lax.all_gather(local_block, axis_name=axis).sum(axis=0)
+
+    return _start_paths(block)
 
 
 def shards(signals, dictionary, selected, inverses):

time: 169 us -> 162 us (0.959)
  blocking collectives: 90.2 us -> 81.6 us
  other arithmetic: 2.78 us -> 6.93 us
  waiting for transfers between devices: 51.7 us -> 48.4 us
    psum x2 -> x0, blocking collectives: 72.6 us -> none  [spread(): return lax.psum(block, axis)]
    all_gather x0 -> x2, blocking collectives: none -> 61.7 us  [_start_paths(): return jax.lax.all_gather(local_block, axis_name=axis).sum(axis=0)]
    psum x1 -> x0, waiting for transfers between devices: 35.7 us -> none  [spread(): return lax.psum(block, axis)]
    all_gather x0 -> x2, waiting for transfers between devices: none -> 32.4 us  [_start_paths(): return jax.lax.all_gather(local_block, axis_name=axis).sum(axis=0)]
    reduce_sum x0 -> x4, other arithmetic: none -> 4.27 us  [_start_paths(): return jax.lax.all_gather(local_block, axis_name=axis).sum(axis=0)]
    pmax x1, blocking collectives: 17.6 us -> 19.9 us  [shards(): largest = lax.pmax(jnp.max(jnp.abs(correlation), axis=0), 'atoms')]
  transfers between devices with their start and end apart: 2 -> 3, of which waited for: 2 -> 3; matrix products, arithmetic and copies ran while one was open for 1% -> 4% of each run, Pallas kernels for 0% -> 0%
where the time goes in v1:
time: 162 us; the launch traced here: 161 us
  blocking collectives  81.6 us (50%)
  waiting for transfers between devices  48.4 us (30%)
  between operations  19.1 us (12%)
  other arithmetic  6.93 us (4%)
  matrix products  3.8 us (2%)
    all_gather x2, blocking collectives, _start_paths(): return jax.lax.all_gather(local_block, axis_name=axis).sum(axis=0)  61.7 us
    all_gather x2, waiting for transfers between devices, _start_paths(): return jax.lax.all_gather(local_block, axis_name=axis).sum(axis=0)  32.4 us
    pmax x1, blocking collectives, shards(): largest = lax.pmax(jnp.max(jnp.abs(correlation), axis=0), 'atoms')  19.9 us
    all_gather x1, waiting for transfers between devices, shards(): gathered = lax.all_gather(dictionary, 'sig', axis=1, tiled=True)  14.6 us
    reduce_sum x4, other arithmetic, _start_paths(): return jax.lax.all_gather(local_block, axis_name=axis).sum(axis=0)  4.27 us
  transfers between devices with their start and end apart: 3, of which 3 were waited for; matrix products, arithmetic and copies ran while one was open for 4% of the time, Pallas kernels for 0%

profile of v1, /device:TPU:0, one launch (start us, length us, event | category | flops | bytes accessed | tf_op | source)
XLA Modules:
  0.0 161.2 jit_solution(10532862490577517941)
XLA Ops:
  7.2 0.0 copy-start
  7.2 0.0 copy-start.2
  7.2 0.0 all-gather.8.cloned.1.call-start
  7.2 0.7 all-gather.8.cloned.1.call-update
  7.9 0.0 all-gather.10.cloned.1.call-start
  8.0 1.3 fusion.12
  14.5 14.6 %all-gather.8.cloned.1.call-done = bf16[1024,512]{1,0:T(8,128)(2,1)} async-done(((bf16[1024,128]{1,0:T(8,128)(2,1)}), bf16[1024,512]{1,0:T(8,128)(2,1)}) %all-gather.8.cloned.1.call-update) | async-done | bytes 1048592 | tf_op jit(solution)/shard_map/all_gather | solution.py:21
  29.1 2.0 %dynamic-slice_select_fusion = (bf16[1024,64]{1,0:T(8,128)(2,1)}, bf16[1024,64]{1,0:T(8,128)(2,1)}) fusion(bf16[1024,512]{1,0:T(8,128)(2,1)} %all-gather.8.cloned.1.call-done, s32[]{:T(128)S(6)} %select_n.99, pred[]{:T(512)S(6)} %eq.16, s32[]{:T(128)S(6)} %select_n.91, pred[]{:T(512)S(6)} %eq.15), kind=kLoop, calls=%fused_computation.11 | loop fusion | flops 131072 | bytes 524298 | tf_op jit(solution)/shard_map/while/body/eval_jaxpr/jit(_where)/select_n | solution.py:12
  31.2 0.0 all-gather.10.cloned.1.call-update
  31.2 0.0 all-gather.12.cloned.1.call-start
  31.3 0.7 all-gather.12.cloned.1.call-update
  32.0 0.0 copy-done
  32.0 0.0 copy-start.1
  32.0 1.8 %fusion.13 = f32[512,128]{1,0:T(8,128)S(1)} fusion(bf16[1024,512]{1,0:T(8,128)(2,1)} %all-gather.8.cloned.1.call-done, bf16[1024,128]{1,0:T(8,128)(2,1)S(1)} %copy-done), kind=kOutput, calls=%fused_computation.23 | convolution fusion | flops 134217728 | bytes 1572864 | tf_op jit(solution)/shard_map/dot_general | solution.py:25
  33.8 0.0 copy-done.2
  33.8 0.2 fusion.1
  33.9 30.8 %all-gather.1 = bf16[512,128]{1,0:T(8,128)(2,1)S(1)} all-gather(bf16[64,128]{1,0:T(8,128)(2,1)S(1)} %fusion.1), channel_id=3, replica_groups=mesh['atoms'=8,'sig'=4] {'atoms'}, dimensions={0}, use_global_device_ids=true | all-gather | bytes 147456 | tf_op jit(solution)/shard_map/while/body/eval_jaxpr/all_gather | solution.py:15
  64.8 15.7 %all-gather.10.cloned.1.call-done = bf16[8192,64]{1,0:T(8,128)(2,1)} async-done(((bf16[1024,64]{1,0:T(8,128)(2,1)}), bf16[8192,64]{1,0:T(8,128)(2,1)}) %all-gather.10.cloned.1.call-update) | async-done | bytes 1048592 | tf_op jit(solution)/shard_map/while/body/eval_jaxpr/all_gather | solution.py:15
  80.5 2.1 %reduce_sum.52 = bf16[1024,64]{1,0:T(8,128)(2,1)S(1)} reduce(bf16[8,1024,64]{2,1,0:T(8,128)(2,1)} %bitcast.27, bf16[]{:T(256)} %constant.95.clone.1), dimensions={0}, to_apply=%region_0.1 | reduce | flops 458752 | bytes 1179650 | tf_op jit(solution)/shard_map/while/body/eval_jaxpr/reduce_sum | solution.py:15
  82.6 0.0 copy-done.1
  82.6 0.5 convolution_subtract_fusion.1
  83.2 0.2 fusion.3
  83.3 30.9 %all-gather.3 = bf16[512,128]{1,0:T(8,128)(2,1)S(1)} all-gather(bf16[64,128]{1,0:T(8,128)(2,1)S(1)} %fusion.3), channel_id=5, replica_groups=mesh['atoms'=8,'sig'=4] {'atoms'}, dimensions={0}, use_global_device_ids=true | all-gather | bytes 147456 | tf_op jit(solution)/shard_map/while/body/eval_jaxpr/all_gather | solution.py:15
  114.2 16.7 %all-gather.12.cloned.1.call-done = bf16[8192,64]{1,0:T(8,128)(2,1)} async-done(((bf16[1024,64]{1,0:T(8,128)(2,1)}), bf16[8192,64]{1,0:T(8,128)(2,1)}) %all-gather.12.cloned.1.call-update) | async-done | bytes 1048592 | tf_op jit(solution)/shard_map/while/body/eval_jaxpr/all_gather | solution.py:15
  130.9 2.1 %reduce_sum.54 = bf16[1024,64]{1,0:T(8,128)(2,1)S(1)} reduce(bf16[8,1024,64]{2,1,0:T(8,128)(2,1)} %bitcast.26, bf16[]{:T(256)} %constant.95.clone.1), dimensions={0}, to_apply=%region_2.3 | reduce | flops 458752 | bytes 1179650 | tf_op jit(solution)/shard_map/while/body/eval_jaxpr/reduce_sum | solution.py:15
  133.0 1.2 abs_reduce_fusion
  134.2 19.9 %pmax.7 = f32[128]{0:T(128)} all-reduce(f32[128]{0:T(128)S(1)} %get-tuple-element.33), channel_id=1, replica_groups=mesh['atoms'=8,'sig'=4] {'atoms'}, use_global_device_ids=true, to_apply=%region_5.6 | all-reduce | flops 128 | bytes 1024 | tf_op jit(solution)/shard_map/pmax | solution.py:80
  154.0 0.6 pad_maximum_fusion
  (2 shorter events, 0.0 us)
Async XLA Ops:
  7.2 24.8 %copy-start = (bf16[1024,128]{1,0:T(8,128)(2,1)S(1)}, bf16[1024,128]{1,0:T(8,128)(2,1)}, u32[]{:S(2)}) copy-start(bf16[1024,128]{1,0:T(8,128)(2,1)} %param.4) | copy-start | bytes 786436
  7.2 26.6 %copy-start.2 = (bf16[2,1,64,64]{3,2,1,0:T(8,128)(2,1)S(1)}, bf16[2,1,64,64]{3,2,1,0:T(8,128)(2,1)}, u32[]{:S(2)}) copy-start(bf16[2,1,64,64]{3,2,1,0:T(8,128)(2,1)} %param.7) | copy-start | bytes 49156
  7.2 22.0 %all-gather.8.cloned.1.call-start = ((), (), s32[]{:S(2)}) async-start(), calls=%async_computation | async-start | bytes 1310720 | tf_op jit(solution)/shard_map/all_gather | solution.py:21
  7.9 72.6 %all-gather.10.cloned.1.call-start = ((), (), s32[]{:S(2)}) async-start(), calls=%async_computation.1 | async-start | bytes 2359296 | tf_op jit(solution)/shard_map/while/body/eval_jaxpr/all_gather | solution.py:15
  31.2 99.6 %all-gather.12.cloned.1.call-start = ((), (), s32[]{:S(2)}) async-start(), calls=%async_computation.2 | async-start | bytes 2359296 | tf_op jit(solution)/shard_map/while/body/eval_jaxpr/all_gather | solution.py:15
  32.0 50.7 %copy-start.1 = (bf16[1024,512]{1,0:T(8,128)(2,1)S(1)}, bf16[1024,512]{1,0:T(8,128)(2,1)}, u32[]{:S(2)}) copy-start(bf16[1024,512]{1,0:T(8,128)(2,1)} %all-gather.8.cloned.1.call-done) | copy-start | bytes 3145732
Sparse Core Ops, SparseCore 0:
  9.6 19.5 all-gather.7
  31.3 49.1 all-gather.9
  82.6 48.1 all-gather.11
